TPU v7x, 256 devices: a whole 4x4x8 slice. The times are simulated.
256 devices in a mesh: section: 2 (over core), dp: 32 (over z, x), mp: 4 (over y).
Axes of the slice: x: 4, y: 4, z: 8, core: 2. Of those that a mesh axis runs over, the one named last changes fastest.
Arguments:
- features: bfloat16 [32768, 4096], P(('section', 'dp'), 'mp'), may hold values from -16 to 16
- w_in: bfloat16 [4096, 2048], P(('section', 'dp'), 'mp'), may hold values from -0.09375 to 0.09375
- w_out: bfloat16 [512, 2048], P(('section', 'dp'), 'mp'), may hold values from -0.125 to 0.125
- codebook: bfloat16 [3, 65536, 512], P(None, ('section', 'dp'), 'mp'), may hold values from -3 to 3
- codes: int32 [3, 32768], P(None, ('section', 'dp')), may hold values from 0 to 65535, as said below
- decoder_grad: bfloat16 [32768, 512], P(('section', 'dp'), 'mp'), may hold values from -16 to 16
Outputs:
- in_grad: float32 [4096, 2048], P(('section', 'dp'), 'mp')
- out_grad: float32 [512, 2048], P(('section', 'dp'), 'mp')
- code_sums: float32 [3, 65536, 512], P(None, ('section', 'dp'), 'mp')
Inputs may be any that keep to these rules, and one draw needn't show every extreme that they name: Row k of a level's codebook belongs to owner k // 1024. Within the 512 items of one device (aligned blocks of items), at each level at most 16 codes belong to one owner; at each level some owner receives exactly 16 codes from every device's items.
All inputs are finite; a program needn't handle non-finite values.
Results may differ from a plain program's by a relative error of at most 0.0026.
Values may be sent and summed in bfloat16 or wider, within the bound.
No kernel may reach another device: no remote copies, remote signals or barrier semaphores. Data moves between devices by JAX's collectives and lax.ppermute only.
A program may use at most 64 MiB of HBM per device.

v0:
```python
import jax
import jax.numpy as jnp
from jax import lax
from jax.sharding import PartitionSpec as P

BETA = 0.25


def silu_slope(preact):
    logistic = jax.nn.sigmoid(preact)
    return logistic * (1.0 + preact * (1.0 - logistic))


def send_requests(outgoing):
    return lax.all_to_all(outgoing, ("section", "dp"), split_axis=0, concat_axis=0, tiled=True)


def send_rows(outgoing):
    return lax.all_to_all(outgoing, ("section", "dp"), split_axis=0, concat_axis=0, tiled=True)


def send_sums(outgoing):
    return lax.all_to_all(outgoing, ("section", "dp"), split_axis=0, concat_axis=0, tiled=True)


def shards(features, w_in, w_out, codebook, codes, decoder_grad):
    owners = lax.axis_size(("section", "dp"))
    item_rows = features.shape[0]
    levels, rows_own, width_part = codebook.shape
    capacity = max(2, 2 * item_rows // owners)
    items_all = item_rows * owners
    all_features = lax.all_gather(features, "mp", axis=1, tiled=True)
    preact = jnp.dot(
        all_features,
        lax.all_gather(w_in, ("section", "dp"), axis=0, tiled=True),
        preferred_element_type=jnp.float32,
    )
    hidden = jax.nn.silu(preact).astype(jnp.bfloat16)
    out_full = lax.all_gather(w_out, ("section", "dp"), axis=0, tiled=True)
    latent_part = lax.dot_general(
        hidden, out_full, (((1,), (1,)), ((), ())), preferred_element_type=jnp.float32
    )
    latent = lax.psum_scatter(latent_part, "mp", scatter_dimension=1, tiled=True)
    owner_of = codes // rows_own
    level_ids = jnp.arange(levels, dtype=jnp.int32)[:, None]
    flat_rows = codes % rows_own + level_ids * rows_own
    matches = (owner_of[:, :, None] == jnp.arange(owners, dtype=jnp.int32)).astype(jnp.int32)
    ranking = jnp.sum(jnp.cumsum(matches, axis=1) * matches, axis=2) - 1
    flat_book = codebook.reshape(levels * rows_own, width_part)
    slot_of = owner_of * capacity + ranking
    requests = (
        jnp.zeros((levels, owners * capacity), jnp.int32).at[level_ids, slot_of].set(flat_rows)
    )
    asked_list = []
    fetched_list = []
    for level_index in range(levels):
        asked_rows = send_requests(requests[level_index].reshape(owners, capacity))
        rows_back = send_rows(jnp.take(flat_book, asked_rows, axis=0))
        asked_list.append(asked_rows)
        fetched_list.append(
            jnp.take(rows_back.reshape(owners * capacity, width_part), slot_of[level_index], axis=0)
        )
    codewords = jnp.stack(fetched_list)
    residual = latent
    pull_sum = jnp.zeros_like(latent)
    inputs = []
    for level_index in range(levels):
        inputs.append(residual)
        residual = residual - codewords[level_index].astype(jnp.float32)
        pull_sum = pull_sum + residual
    code_total = jnp.zeros((levels * rows_own, width_part), jnp.float32)
    for level_index in range(levels):
        outgoing = (
            jnp.zeros((owners * capacity, width_part), jnp.float32)
            .at[slot_of[level_index]]
            .set(inputs[level_index])
        )
        incoming = send_sums(outgoing.reshape(owners, capacity, width_part))
        code_total = code_total.at[asked_list[level_index].reshape(-1)].add(
            incoming.reshape(-1, width_part)
        )
    code_sums = code_total.reshape(levels, rows_own, width_part)
    latent_grad = (
        (decoder_grad.astype(jnp.float32) + 2.0 * BETA * pull_sum)
        / jnp.sqrt(jnp.float32(items_all))
    ).astype(jnp.bfloat16)
    grad_full = lax.all_gather(latent_grad, "mp", axis=1, tiled=True)
    out_grad = lax.psum_scatter(
        lax.dot_general(
            grad_full, hidden, (((0,), (0,)), ((), ())), preferred_element_type=jnp.float32
        ),
        ("section", "dp"),
        scatter_dimension=0,
        tiled=True,
    )
    back_hidden = jnp.dot(grad_full, out_full, preferred_element_type=jnp.float32)
    pre_grad = (back_hidden * silu_slope(preact)).astype(jnp.bfloat16)
    in_grad = lax.psum_scatter(
        lax.dot_general(
            all_features, pre_grad, (((0,), (0,)), ((), ())), preferred_element_type=jnp.float32
        ),
        ("section", "dp"),
        scatter_dimension=0,
        tiled=True,
    )
    return (in_grad, out_grad, code_sums)


def solution(mesh):
    in_specs = (
        P(("section", "dp"), "mp"),
        P(("section", "dp"), "mp"),
        P(("section", "dp"), "mp"),
        P(None, ("section", "dp"), "mp"),
        P(None, ("section", "dp")),
        P(("section", "dp"), "mp"),
    )
    out_specs = (
        P(("section", "dp"), "mp"),
        P(("section", "dp"), "mp"),
        P(None, ("section", "dp"), "mp"),
    )
    return jax.shard_map(shards, mesh=mesh, in_specs=in_specs, out_specs=out_specs, check_vma=False)
```

profile of v0, /device:TPU:8, one launch (start us, length us, event | category | flops | bytes accessed | tf_op | source)
XLA Modules:
  0.0 587.1 jit_solution(6716186569917230961)
XLA Ops:
  7.2 0.7 all-gather.3.cloned.1.call-update
  8.0 0.7 all-gather.5.cloned.1.call-update
  8.7 0.8 fusion.17
  9.5 3.6 reduce-window.6
  13.1 0.4 slice_reduce_fusion
  13.6 0.2 fusion.9
  13.8 0.7 multiply_reduce_fusion
  14.6 0.7 and_reduce_fusion
  15.3 6.2 %scatter_custom_fusion.6 = s32[3072]{0:T(1024)S(1)} fusion(s32[1536]{0:T(1024)S(1)} %reshape.377, s32[1536]{0:T(1024)S(1)} %reshape.379, s32[]{:T(128)} %constant.45.clone.1), kind=kCustom, calls=%fused_computation.72 | custom fusion | bytes 12292
  21.5 0.7 all_to_all.46
  22.2 11.9 %all-to-all-start.2 = ((s32[64,1,16]{2,1,0:T(1,128)}), s32[64,1,16]{2,1,0:T(1,128)S(1)}, u32[]{:S(2)}, u32[]{:S(2)}) async-start(s32[64,1,16]{2,1,0:T(1,128)} %bitcast.9), calls=%async_computation.3 | async-start | bytes 65536 | tf_op jit(solution)/shard_map/all_to_all | solution.py:15
  34.2 129.8 %all_gather.14 = bf16[512,512]{1,0:T(8,128)(2,1)S(1)} all-gather(bf16[8,512]{1,0:T(8,128)(2,1)} %param.12), channel_id=1, replica_groups=mesh['section'=2,'dp'=32,'mp'=4] {'section','dp'}, dimensions={0}, use_global_device_ids=true | all-gather | bytes 532480 | tf_op jit(solution)/shard_map/all_gather | solution.py:39
  164.1 0.7 all_to_all.42
  164.8 0.7 all_to_all.50
  165.5 19.5 %all-to-all-start.4 = ((s32[64,1,16]{2,1,0:T(1,128)}), s32[64,1,16]{2,1,0:T(1,128)S(1)}, u32[]{:S(2)}, u32[]{:S(2)}) async-start(s32[64,1,16]{2,1,0:T(1,128)} %bitcast.14), calls=%async_computation.5 | async-start | bytes 65536 | tf_op jit(solution)/shard_map/all_to_all | solution.py:15
  185.0 0.1 reshape.398
  185.1 9.1 %all-to-all-done.4 = s32[64,1,16]{2,1,0:T(1,128)S(1)} async-done(((s32[64,1,16]{2,1,0:T(1,128)}), s32[64,1,16]{2,1,0:T(1,128)S(1)}, u32[]{:S(2)}, u32[]{:S(2)}) %all-to-all-start.4) | async-done | bytes 4128 | tf_op jit(solution)/shard_map/all_to_all | solution.py:15
  194.2 4.6 all-to-all-start
  198.8 0.1 reshape.404
  198.9 3.2 gather_fusion.4
  202.2 0.9 broadcast_select_fusion
  203.1 6.8 %multiply_convert_fusion = (bf16[512,512]{1,0:T(8,128)(2,1)S(1)}, f32[512,512]{1,0:T(8,128)}) fusion(bf16[512,4096]{1,0:T(8,128)(2,1)} %all-gather.3.cloned.1.call-done, bf16[4096,512]{1,0:T(8,128)(2,1)} %all-gather.5.cloned.1.call-done), kind=kOutput, calls=%fused_computation.20 | convolution fusion | flops 2148794368 | bytes 9961472 | tf_op jit(solution)/shard_map/dot_general | solution.py:33
  209.9 1.4 fusion.25
  211.4 10.2 %all-to-all-start.5 = ((bf16[64,16,128]{2,1,0:T(8,128)(2,1)}), bf16[64,16,128]{2,1,0:T(8,128)(2,1)S(1)}, u32[]{:S(2)}, u32[]{:S(2)}) async-start(bf16[64,16,128]{2,1,0:T(8,128)(2,1)} %broadcast_select_fusion), calls=%async_computation.6 | async-start | bytes 524288 | tf_op jit(solution)/shard_map/all_to_all | solution.py:19
  221.7 3.2 gather_fusion.2
  224.9 0.9 broadcast_select_fusion.1
  225.9 7.6 %all-to-all-done.5 = bf16[64,16,128]{2,1,0:T(8,128)(2,1)S(1)} async-done(((bf16[64,16,128]{2,1,0:T(8,128)(2,1)}), bf16[64,16,128]{2,1,0:T(8,128)(2,1)S(1)}, u32[]{:S(2)}, u32[]{:S(2)}) %all-to-all-start.5) | async-done | bytes 262176 | tf_op jit(solution)/shard_map/all_to_all | solution.py:19
  233.5 6.0 %all-to-all-start.3 = ((bf16[64,16,128]{2,1,0:T(8,128)(2,1)}), bf16[64,16,128]{2,1,0:T(8,128)(2,1)S(1)}, u32[]{:S(2)}, u32[]{:S(2)}) async-start(bf16[64,16,128]{2,1,0:T(8,128)(2,1)} %broadcast_select_fusion.1), calls=%async_computation.4 | async-start | bytes 524288 | tf_op jit(solution)/shard_map/all_to_all | solution.py:19
  239.5 3.2 gather_fusion
  242.7 0.9 broadcast_select_fusion.2
  243.6 7.7 %all-to-all-done.3 = bf16[64,16,128]{2,1,0:T(8,128)(2,1)S(1)} async-done(((bf16[64,16,128]{2,1,0:T(8,128)(2,1)}), bf16[64,16,128]{2,1,0:T(8,128)(2,1)S(1)}, u32[]{:S(2)}, u32[]{:S(2)}) %all-to-all-start.3) | async-done | bytes 262176 | tf_op jit(solution)/shard_map/all_to_all | solution.py:19
  251.4 6.0 %all-to-all-start.1 = ((bf16[64,16,128]{2,1,0:T(8,128)(2,1)}), bf16[64,16,128]{2,1,0:T(8,128)(2,1)S(1)}, u32[]{:S(2)}, u32[]{:S(2)}) async-start(bf16[64,16,128]{2,1,0:T(8,128)(2,1)} %broadcast_select_fusion.2), calls=%async_computation.2 | async-start | bytes 524288 | tf_op jit(solution)/shard_map/all_to_all | solution.py:19
  257.3 0.2 reduce-scatter.8.cloned.1.call-start
  257.6 1.3 gather_fusion.5
  259.0 1.3 gather_fusion.3
  260.3 8.9 %all-to-all-done.1 = bf16[64,16,128]{2,1,0:T(8,128)(2,1)S(1)} async-done(((bf16[64,16,128]{2,1,0:T(8,128)(2,1)}), bf16[64,16,128]{2,1,0:T(8,128)(2,1)S(1)}, u32[]{:S(2)}, u32[]{:S(2)}) %all-to-all-start.1) | async-done | bytes 262176 | tf_op jit(solution)/shard_map/all_to_all | solution.py:19
  269.2 1.3 gather_fusion.1
  270.6 1.2 multiply_convert_fusion.1
  271.8 14.5 %all_gather.15 = bf16[512,512]{1,0:T(8,128)(2,1)S(1)} all-gather(bf16[512,128]{1,0:T(8,128)(2,1)S(1)} %multiply_convert_fusion.1), channel_id=1, replica_groups=mesh['section'=2,'dp'=32,'mp'=4] {'mp'}, dimensions={1}, use_global_device_ids=true | all-gather | bytes 655360 | tf_op jit(solution)/shard_map/all_gather | solution.py:87
  286.3 1.5 fusion.26
  287.8 8.6 %convolution_bitcast_fusion = f32[4096,512]{0,1:T(8,128)} fusion(bf16[512,4096]{1,0:T(8,128)(2,1)} %all-gather.3.cloned.1.call-done, bf16[512,512]{1,0:T(8,128)(2,1)S(1)} %all_gather.15, bf16[512,512]{1,0:T(8,128)(2,1)S(1)} %all_gather.14, f32[512,512]{1,0:T(8,128)} %get-tuple-element.28), kind=kOutput, calls=%fused_computation.13 | convolution fusion | flops 2418278400 | bytes 14680064 | tf_op jit(solution)/shard_map/dot_general | solution.py:99
  296.4 9.0 %copy.17 = f32[4096,512]{1,0:T(8,128)} copy(f32[4096,512]{0,1:T(8,128)} %convolution_bitcast_fusion) | data formatting | bytes 16777216
  305.5 0.9 copy-done.2
  306.4 2.7 scatter_custom_fusion.2
  309.1 5.9 %all-to-all-start.7 = ((f32[64,16,128]{2,1,0:T(8,128)}), f32[64,16,128]{2,1,0:T(8,128)S(1)}, u32[]{:S(2)}, u32[]{:S(2)}) async-start(f32[64,16,128]{2,1,0:T(8,128)} %bitcast.27), calls=%async_computation.9 | async-start | bytes 1048576 | tf_op jit(solution)/shard_map/all_to_all | solution.py:23
  315.0 2.5 scatter_custom_fusion
  317.5 14.3 %all-to-all-done.7 = f32[64,16,128]{2,1,0:T(8,128)S(1)} async-done(((f32[64,16,128]{2,1,0:T(8,128)}), f32[64,16,128]{2,1,0:T(8,128)S(1)}, u32[]{:S(2)}, u32[]{:S(2)}) %all-to-all-start.7) | async-done | bytes 524320 | tf_op jit(solution)/shard_map/all_to_all | solution.py:23
  331.8 6.6 %all-to-all-start.6 = ((f32[64,16,128]{2,1,0:T(8,128)}), f32[64,16,128]{2,1,0:T(8,128)S(1)}, u32[]{:S(2)}, u32[]{:S(2)}) async-start(f32[64,16,128]{2,1,0:T(8,128)} %bitcast.22), calls=%async_computation.8 | async-start | bytes 1048576 | tf_op jit(solution)/shard_map/all_to_all | solution.py:23
  338.4 2.7 scatter_custom_fusion.4
  341.1 14.1 %all-to-all-done.6 = f32[64,16,128]{2,1,0:T(8,128)S(1)} async-done(((f32[64,16,128]{2,1,0:T(8,128)}), f32[64,16,128]{2,1,0:T(8,128)S(1)}, u32[]{:S(2)}, u32[]{:S(2)}) %all-to-all-start.6) | async-done | bytes 524320 | tf_op jit(solution)/shard_map/all_to_all | solution.py:23
  355.2 6.8 %all-to-all-start.8 = ((f32[64,16,128]{2,1,0:T(8,128)}), f32[64,16,128]{2,1,0:T(8,128)S(1)}, u32[]{:S(2)}, u32[]{:S(2)}) async-start(f32[64,16,128]{2,1,0:T(8,128)} %bitcast.32), calls=%async_computation.10 | async-start | bytes 1048576 | tf_op jit(solution)/shard_map/all_to_all | solution.py:23
  362.0 0.5 broadcast.241
  362.5 0.7 reduce.15
  363.2 0.1 reshape.261
  363.3 0.7 reduce.16
  364.1 0.1 reshape.264
  364.1 0.7 reduce.17
  364.9 0.1 reshape.267
  365.0 6.8 %scatter_custom_fusion.1 = f32[3072,128]{1,0:T(8,128)S(1)} fusion(s32[1024]{0:T(1024)S(1)} %bitcast.95, f32[1024,128]{1,0:T(8,128)} %bitcast.80, f32[]{:T(128)} %constant.79.clone.1), kind=kCustom, calls=%fused_computation.22 | custom fusion | flops 131072 | bytes 1573376 | tf_op jit(solution)/shard_map/scatter-add | solution.py:79
  371.8 6.6 %scatter_fusion = f32[3072,128]{1,0:T(8,128)S(1)} fusion(f32[3072,128]{1,0:T(8,128)S(1)} %scatter_custom_fusion.1, s32[1024]{0:T(1024)S(1)} %bitcast.94, f32[1024,128]{1,0:T(8,128)S(1)} %bitcast.75), kind=kCustom, calls=%fused_computation.9 | custom fusion | flops 131072 | bytes 1576960 | tf_op jit(solution)/shard_map/scatter-add | solution.py:79
  378.5 1.5 all-to-all-done.8
  380.0 6.6 %scatter_fusion.1 = f32[3072,128]{1,0:T(8,128)S(1)} fusion(f32[3072,128]{1,0:T(8,128)S(1)} %scatter_fusion, s32[1024]{0:T(1024)S(1)} %bitcast.93, f32[1024,128]{1,0:T(8,128)S(1)} %bitcast.76), kind=kCustom, calls=%fused_computation.11 | custom fusion | flops 131072 | bytes 1576960 | tf_op jit(solution)/shard_map/scatter-add | solution.py:79
  386.6 38.4 %reduce-scatter.8.cloned.1.call-done = f32[8,512]{1,0:T(8,128)} async-done(((f32[512,512]{1,0:T(8,128)}), f32[8,512]{1,0:T(8,128)}) %reduce-scatter.8.cloned.1.call-update) | async-done | bytes 16400 | tf_op jit(solution)/shard_map/reduce_scatter | solution.py:88
  425.0 155.6 %reduce-scatter.10.cloned.1.call-done = f32[64,512]{1,0:T(8,128)} async-done(((f32[4096,512]{1,0:T(8,128)}), f32[64,512]{1,0:T(8,128)}) %reduce-scatter.10.cloned.1.call-update) | async-done | bytes 131088
  (55 shorter events, 0.6 us)
Async XLA Ops:
  7.2 191.8 %copy-start = (bf16[3,1024,128]{2,1,0:T(8,128)(2,1)S(1)}, bf16[3,1024,128]{2,1,0:T(8,128)(2,1)}, u32[]{:S(2)}) copy-start(bf16[3,1024,128]{2,1,0:T(8,128)(2,1)} %param.13) | copy-start | bytes 2359300
  7.2 195.9 %all-gather.3.cloned.1.call-start = ((), (), s32[]{:S(2)}) async-start(), calls=%async_computation.12 | async-start | bytes 5242880 | tf_op jit(solution)/shard_map/all_gather | solution.py:32
  7.9 195.2 %all-gather.5.cloned.1.call-start = ((), (), s32[]{:S(2)}) async-start(), calls=%async_computation.13 | async-start | bytes 4259840 | tf_op jit(solution)/shard_map/all_gather | solution.py:35
  22.2 143.2 %all-to-all-start.2 = ((s32[64,1,16]{2,1,0:T(1,128)}), s32[64,1,16]{2,1,0:T(1,128)S(1)}, u32[]{:S(2)}, u32[]{:S(2)}) async-start(s32[64,1,16]{2,1,0:T(1,128)} %bitcast.9), calls=%async_computation.3 | async-start | bytes 65536 | tf_op jit(solution)/shard_map/all_to_all | solution.py:15
  165.5 28.8 %all-to-all-start.4 = ((s32[64,1,16]{2,1,0:T(1,128)}), s32[64,1,16]{2,1,0:T(1,128)S(1)}, u32[]{:S(2)}, u32[]{:S(2)}) async-start(s32[64,1,16]{2,1,0:T(1,128)} %bitcast.14), calls=%async_computation.5 | async-start | bytes 65536 | tf_op jit(solution)/shard_map/all_to_all | solution.py:15
  194.2 17.2 %all-to-all-start = ((s32[64,1,16]{2,1,0:T(1,128)}), s32[64,1,16]{2,1,0:T(1,128)S(1)}, u32[]{:S(2)}, u32[]{:S(2)}) async-start(s32[64,1,16]{2,1,0:T(1,128)} %bitcast.3), calls=%async_computation.1 | async-start | bytes 65536 | tf_op jit(solution)/shard_map/all_to_all | solution.py:15
  198.8 71.8 %reduce-scatter.6.cloned.1.call-start = ((), (), s32[]{:S(2)}) async-start(), calls=%async_computation.14 | async-start | bytes 1310720 | tf_op jit(solution)/shard_map/reduce_scatter | solution.py:43
  211.4 22.1 %all-to-all-start.5 = ((bf16[64,16,128]{2,1,0:T(8,128)(2,1)}), bf16[64,16,128]{2,1,0:T(8,128)(2,1)S(1)}, u32[]{:S(2)}, u32[]{:S(2)}) async-start(bf16[64,16,128]{2,1,0:T(8,128)(2,1)} %broadcast_select_fusion), calls=%async_computation.6 | async-start | bytes 524288 | tf_op jit(solution)/shard_map/all_to_all | solution.py:19
  224.9 45.7 %copy-start.4 = (bf16[512,128]{1,0:T(8,128)(2,1)S(1)}, bf16[512,128]{1,0:T(8,128)(2,1)}, u32[]{:S(2)}) copy-start(bf16[512,128]{1,0:T(8,128)(2,1)} %param.15) | copy-start | bytes 393220
  233.5 17.9 %all-to-all-start.3 = ((bf16[64,16,128]{2,1,0:T(8,128)(2,1)}), bf16[64,16,128]{2,1,0:T(8,128)(2,1)S(1)}, u32[]{:S(2)}, u32[]{:S(2)}) async-start(bf16[64,16,128]{2,1,0:T(8,128)(2,1)} %broadcast_select_fusion.1), calls=%async_computation.4 | async-start | bytes 524288 | tf_op jit(solution)/shard_map/all_to_all | solution.py:19
  251.4 17.9 %all-to-all-start.1 = ((bf16[64,16,128]{2,1,0:T(8,128)(2,1)}), bf16[64,16,128]{2,1,0:T(8,128)(2,1)S(1)}, u32[]{:S(2)}, u32[]{:S(2)}) async-start(bf16[64,16,128]{2,1,0:T(8,128)(2,1)} %broadcast_select_fusion.2), calls=%async_computation.2 | async-start | bytes 524288 | tf_op jit(solution)/shard_map/all_to_all | solution.py:19
  257.3 167.7 %reduce-scatter.8.cloned.1.call-start = ((), (), s32[]{:S(2)}) async-start(), calls=%async_computation.15 | async-start | bytes 1064960 | tf_op jit(solution)/shard_map/reduce_scatter | solution.py:88
  287.8 292.8 %reduce-scatter.10.cloned.1.call-start = ((), (), s32[]{:S(2)}) async-start(), calls=%async_computation.16 | async-start | bytes 8519680
  305.5 1.0 copy-start.2
  309.1 22.7 %all-to-all-start.7 = ((f32[64,16,128]{2,1,0:T(8,128)}), f32[64,16,128]{2,1,0:T(8,128)S(1)}, u32[]{:S(2)}, u32[]{:S(2)}) async-start(f32[64,16,128]{2,1,0:T(8,128)} %bitcast.27), calls=%async_computation.9 | async-start | bytes 1048576 | tf_op jit(solution)/shard_map/all_to_all | solution.py:23
  331.8 23.4 %all-to-all-start.6 = ((f32[64,16,128]{2,1,0:T(8,128)}), f32[64,16,128]{2,1,0:T(8,128)S(1)}, u32[]{:S(2)}, u32[]{:S(2)}) async-start(f32[64,16,128]{2,1,0:T(8,128)} %bitcast.22), calls=%async_computation.8 | async-start | bytes 1048576 | tf_op jit(solution)/shard_map/all_to_all | solution.py:23
  355.2 9.8 %copy-start.3 = (f32[64,16,128]{2,1,0:T(8,128)}, f32[64,16,128]{2,1,0:T(8,128)S(1)}, u32[]{:S(2)}) copy-start(f32[64,16,128]{2,1,0:T(8,128)S(1)} %all-to-all-done.6) | copy-start | bytes 1572868
  355.2 24.8 %all-to-all-start.8 = ((f32[64,16,128]{2,1,0:T(8,128)}), f32[64,16,128]{2,1,0:T(8,128)S(1)}, u32[]{:S(2)}, u32[]{:S(2)}) async-start(f32[64,16,128]{2,1,0:T(8,128)} %bitcast.32), calls=%async_computation.10 | async-start | bytes 1048576 | tf_op jit(solution)/shard_map/all_to_all | solution.py:23
  386.6 194.0 %copy-start.1 = (f32[3072,128]{1,0:T(8,128)}, f32[3072,128]{1,0:T(8,128)S(1)}, u32[]{:S(2)}) copy-start(f32[3072,128]{1,0:T(8,128)S(1)} %scatter_fusion.1) | copy-start | bytes 4718596
Sparse Core Ops, SparseCore 0:
  9.8 52.9 all-gather.2
  65.6 79.9 all-gather.4
  211.5 24.9 reduce-scatter.5
  287.9 137.0 reduce-scatter.7
  429.6 150.8 reduce-scatter.9
where the time goes:
time: 588 us; the launch traced here: 587 us
  waiting for transfers between devices  259 us (44%)
  blocking collectives  144 us (24%)
  starting transfers between devices  77.8 us (13%)
  other arithmetic  37.9 us (6%)
  local copies, waits for them, and re-layouts  35.8 us (6%)
  matrix products  18.3 us (3%)
  between operations  14.2 us (2%)
    unnamed x6, waiting for transfers between devices  157 us
    all_gather x1, blocking collectives, shards(): out_full = lax.all_gather(w_out, ('section', 'dp'), axis=0, tiled=True)  130 us
    reduce_scatter x1, waiting for transfers between devices, shards(): lax.psum_scatter(lax.dot_general(grad_full, hidden, (((0,), (0,)), ((), (...  38.4 us
    all_to_all x3, starting transfers between devices, send_requests(): lax.all_to_all(outgoing, ('section', 'dp'), split_axis=0, concat_axis=0,...  36 us
    all_to_all x3, waiting for transfers between devices, send_sums(): lax.all_to_all(outgoing, ('section', 'dp'), split_axis=0, concat_axis=0,...  29.9 us
    all_to_all x3, waiting for transfers between devices, send_rows(): lax.all_to_all(outgoing, ('section', 'dp'), split_axis=0, concat_axis=0,...  24.3 us
    all_to_all x3, starting transfers between devices, send_rows(): lax.all_to_all(outgoing, ('section', 'dp'), split_axis=0, concat_axis=0,...  22.1 us
    scatter-add x3, other arithmetic, shards(): code_total.at[asked_list[level_index].reshape(-1)]  20.1 us
  transfers between devices with their start and end apart: 14, of which 9 were waited for; matrix products, arithmetic and copies ran while one was open for 15% of the time, Pallas kernels for 0%

commit v1 on v0

--- a/solution.py
+++ b/solution.py
@@ -36,7 +36,10 @@
         preferred_element_type=jnp.float32,
     )
     hidden = jax.nn.silu(preact).astype(jnp.bfloat16)
-    out_full = lax.all_gather(w_out, ("section", "dp"), axis=0, tiled=True)
+    size = lax.axis_size(("section", "dp"))
+    blocks = jnp.stack([w_out for _ in range(size)])
+    blocks = lax.all_to_all(blocks, ("section", "dp"), split_axis=0, concat_axis=0)
+    out_full = jnp.concatenate(blocks, axis=0)
     latent_part = lax.dot_general(
         hidden, out_full, (((1,), (1,)), ((), ())), preferred_element_type=jnp.float32
     )

time: 588 us -> 540 us (0.918)
  blocking collectives: 144 us -> 14.5 us
  waiting for transfers between devices: 259 us -> 352 us
  starting transfers between devices: 77.8 us -> 63.7 us
    all_gather x1 -> x0, blocking collectives: 130 us -> none  [shards(): out_full = lax.all_gather(w_out, ('section', 'dp'), axis=0, tiled=True)]
    all_gather x1, waiting for transfers between devices: 0.01 us -> 77.9 us  [shards(): lax.all_gather(w_in, ('section', 'dp'), axis=0, tiled=True)]
    all_to_all x3, waiting for transfers between devices: 9.15 us -> 24.7 us  [send_requests(): lax.all_to_all(outgoing, ('section', 'dp'), split_axis=0, concat_axis=0,...]
    all_to_all x3, starting transfers between devices: 36 us -> 22.9 us  [send_requests(): lax.all_to_all(outgoing, ('section', 'dp'), split_axis=0, concat_axis=0,...]
    unnamed x13 -> x17, local copies, waits for them, and re-layouts: 16.2 us -> 16.2 us
  transfers between devices with their start and end apart: 14 -> 15, of which waited for: 9 -> 12; matrix products, arithmetic and copies ran while one was open for 15% -> 16% of each run, Pallas kernels for 0% -> 0%
where the time goes in v1:
time: 540 us; the launch traced here: 538 us
  waiting for transfers between devices  352 us (65%)
  starting transfers between devices  63.7 us (12%)
  other arithmetic  37.9 us (7%)
  local copies, waits for them, and re-layouts  37.4 us (7%)
  matrix products  18.3 us (3%)
  blocking collectives  14.5 us (3%)
  between operations  14.3 us (3%)
    unnamed x6, waiting for transfers between devices  157 us
    all_gather x1, waiting for transfers between devices, shards(): lax.all_gather(w_in, ('section', 'dp'), axis=0, tiled=True)  77.9 us
    reduce_scatter x1, waiting for transfers between devices, shards(): lax.psum_scatter(lax.dot_general(grad_full, hidden, (((0,), (0,)), ((), (...  38.5 us
    all_to_all x3, waiting for transfers between devices, send_sums(): lax.all_to_all(outgoing, ('section', 'dp'), split_axis=0, concat_axis=0,...  30.1 us
    all_to_all x3, waiting for transfers between devices, send_requests(): lax.all_to_all(outgoing, ('section', 'dp'), split_axis=0, concat_axis=0,...  24.7 us
    all_to_all x3, waiting for transfers between devices, send_rows(): lax.all_to_all(outgoing, ('section', 'dp'), split_axis=0, concat_axis=0,...  24.4 us
    all_to_all x3, starting transfers between devices, send_requests(): lax.all_to_all(outgoing, ('section', 'dp'), split_axis=0, concat_axis=0,...  22.9 us
    scatter-add x3, other arithmetic, shards(): code_total.at[asked_list[level_index].reshape(-1)]  20.1 us
  transfers between devices with their start and end apart: 15, of which 12 were waited for; matrix products, arithmetic and copies ran while one was open for 16% of the time, Pallas kernels for 0%

profile of v1, /device:TPU:8, one launch (start us, length us, event | category | flops | bytes accessed | tf_op | source)
XLA Modules:
  0.0 538.5 jit_solution(9360464335784851724)
XLA Ops:
  7.2 0.7 all-gather.3.cloned.1.call-update
  8.0 0.7 all-gather.5.cloned.1.call-update
  8.7 0.8 fusion.21
  9.5 3.6 reduce-window.6
  13.1 0.4 slice_reduce_fusion
  13.6 0.2 fusion.13
  13.8 0.7 multiply_reduce_fusion
  14.6 0.7 and_reduce_fusion
  15.3 6.2 %scatter_custom_fusion.6 = s32[3072]{0:T(1024)S(1)} fusion(s32[1536]{0:T(1024)S(1)} %reshape.383, s32[1536]{0:T(1024)S(1)} %reshape.385, s32[]{:T(128)} %constant.45.clone.1), kind=kCustom, calls=%fused_computation.75 | custom fusion | bytes 12292
  21.5 0.7 all_to_all.54
  22.2 11.9 %all-to-all-start.5 = ((s32[64,1,16]{2,1,0:T(1,128)}), s32[64,1,16]{2,1,0:T(1,128)S(1)}, u32[]{:S(2)}, u32[]{:S(2)}) async-start(s32[64,1,16]{2,1,0:T(1,128)} %bitcast.15), calls=%async_computation.6 | async-start | bytes 65536 | tf_op jit(solution)/shard_map/all_to_all | solution.py:15
  34.2 0.7 all_to_all.46
  34.9 0.7 all_to_all.50
  35.6 7.8 %all-to-all-done.5 = s32[64,1,16]{2,1,0:T(1,128)S(1)} async-done(((s32[64,1,16]{2,1,0:T(1,128)}), s32[64,1,16]{2,1,0:T(1,128)S(1)}, u32[]{:S(2)}, u32[]{:S(2)}) %all-to-all-start.5) | async-done | bytes 4128 | tf_op jit(solution)/shard_map/all_to_all | solution.py:15
  43.4 4.6 all-to-all-start.3
  48.1 9.1 %all-to-all-done.3 = s32[64,1,16]{2,1,0:T(1,128)S(1)} async-done(((s32[64,1,16]{2,1,0:T(1,128)}), s32[64,1,16]{2,1,0:T(1,128)S(1)}, u32[]{:S(2)}, u32[]{:S(2)}) %all-to-all-start.3) | async-done | bytes 4128 | tf_op jit(solution)/shard_map/all_to_all | solution.py:15
  57.2 1.5 stack.2
  58.8 4.6 all-to-all-start
  63.5 3.2 gather_fusion.4
  66.7 0.9 broadcast_select_fusion
  67.6 77.9 %all-gather.5.cloned.1.call-done = bf16[4096,512]{1,0:T(8,128)(2,1)} async-done(((bf16[64,512]{1,0:T(8,128)(2,1)}), bf16[4096,512]{1,0:T(8,128)(2,1)}) %all-gather.5.cloned.1.call-update) | async-done | bytes 4194320 | tf_op jit(solution)/shard_map/all_gather | solution.py:35
  145.5 5.8 %fusion.30 = f32[512,512]{1,0:T(8,128)S(1)} fusion(bf16[512,4096]{1,0:T(8,128)(2,1)} %all-gather.3.cloned.1.call-done, bf16[4096,512]{1,0:T(8,128)(2,1)} %all-gather.5.cloned.1.call-done), kind=kOutput, calls=%fused_computation.96 | convolution fusion | flops 2147483648 | bytes 9437184 | tf_op jit(solution)/shard_map/dot_general | solution.py:33
  151.3 6.3 %all-to-all-start.1 = ((s32[64,1,16]{2,1,0:T(1,128)}), s32[64,1,16]{2,1,0:T(1,128)S(1)}, u32[]{:S(2)}, u32[]{:S(2)}) async-start(s32[64,1,16]{2,1,0:T(1,128)} %bitcast.4), calls=%async_computation.2 | async-start | bytes 65536 | tf_op jit(solution)/shard_map/all_to_all | solution.py:15
  157.7 1.5 fusion.9
  159.2 7.8 %all-to-all-done.1 = s32[64,1,16]{2,1,0:T(1,128)S(1)} async-done(((s32[64,1,16]{2,1,0:T(1,128)}), s32[64,1,16]{2,1,0:T(1,128)S(1)}, u32[]{:S(2)}, u32[]{:S(2)}) %all-to-all-start.1) | async-done | bytes 4128 | tf_op jit(solution)/shard_map/all_to_all | solution.py:15
  167.0 4.6 all-to-all-start.6
  171.7 3.2 gather_fusion.2
  175.0 0.9 broadcast_select_fusion.1
  175.9 7.6 %all-to-all-done.6 = bf16[64,16,128]{2,1,0:T(8,128)(2,1)S(1)} async-done(((bf16[64,16,128]{2,1,0:T(8,128)(2,1)}), bf16[64,16,128]{2,1,0:T(8,128)(2,1)S(1)}, u32[]{:S(2)}, u32[]{:S(2)}) %all-to-all-start.6) | async-done | bytes 262176 | tf_op jit(solution)/shard_map/all_to_all | solution.py:19
  183.5 6.0 %all-to-all-start.4 = ((bf16[64,16,128]{2,1,0:T(8,128)(2,1)}), bf16[64,16,128]{2,1,0:T(8,128)(2,1)S(1)}, u32[]{:S(2)}, u32[]{:S(2)}) async-start(bf16[64,16,128]{2,1,0:T(8,128)(2,1)} %broadcast_select_fusion.1), calls=%async_computation.5 | async-start | bytes 524288 | tf_op jit(solution)/shard_map/all_to_all | solution.py:19
  189.5 3.2 gather_fusion
  192.7 0.9 broadcast_select_fusion.2
  193.7 7.7 %all-to-all-done.4 = bf16[64,16,128]{2,1,0:T(8,128)(2,1)S(1)} async-done(((bf16[64,16,128]{2,1,0:T(8,128)(2,1)}), bf16[64,16,128]{2,1,0:T(8,128)(2,1)S(1)}, u32[]{:S(2)}, u32[]{:S(2)}) %all-to-all-start.4) | async-done | bytes 262176 | tf_op jit(solution)/shard_map/all_to_all | solution.py:19
  201.4 6.0 %all-to-all-start.2 = ((bf16[64,16,128]{2,1,0:T(8,128)(2,1)}), bf16[64,16,128]{2,1,0:T(8,128)(2,1)S(1)}, u32[]{:S(2)}, u32[]{:S(2)}) async-start(bf16[64,16,128]{2,1,0:T(8,128)(2,1)} %broadcast_select_fusion.2), calls=%async_computation.3 | async-start | bytes 524288 | tf_op jit(solution)/shard_map/all_to_all | solution.py:19
  207.4 1.3 gather_fusion.5
  208.8 1.3 gather_fusion.3
  210.1 9.1 %all-to-all-done.2 = bf16[64,16,128]{2,1,0:T(8,128)(2,1)S(1)} async-done(((bf16[64,16,128]{2,1,0:T(8,128)(2,1)}), bf16[64,16,128]{2,1,0:T(8,128)(2,1)S(1)}, u32[]{:S(2)}, u32[]{:S(2)}) %all-to-all-start.2) | async-done | bytes 262176 | tf_op jit(solution)/shard_map/all_to_all | solution.py:19
  219.2 1.3 gather_fusion.1
  220.6 1.2 multiply_convert_fusion.1
  221.9 14.5 %all_gather.11 = bf16[512,512]{1,0:T(8,128)(2,1)S(1)} all-gather(bf16[512,128]{1,0:T(8,128)(2,1)S(1)} %multiply_convert_fusion.1), channel_id=1, replica_groups=mesh['section'=2,'dp'=32,'mp'=4] {'mp'}, dimensions={1}, use_global_device_ids=true | all-gather | bytes 655360 | tf_op jit(solution)/shard_map/all_gather | solution.py:90
  236.3 2.8 fusion.27
  239.2 8.3 %convolution_bitcast_fusion = f32[4096,512]{0,1:T(8,128)} fusion(bf16[512,4096]{1,0:T(8,128)(2,1)} %all-gather.3.cloned.1.call-done, bf16[512,512]{1,0:T(8,128)(2,1)S(1)} %all_gather.11, f32[512,512]{1,0:T(8,128)S(1)} %copy-done.6, bf16[64,8,512]{2,1,0:T(8,128)(2,1)S(1)} %all-to-all-done), kind=kOutput, calls=%fused_computation.13 | convolution fusion | flops 2418278400 | bytes 14680064 | tf_op jit(solution)/shard_map/dot_general | solution.py:102
  247.5 9.0 %copy.17 = f32[4096,512]{1,0:T(8,128)} copy(f32[4096,512]{0,1:T(8,128)} %convolution_bitcast_fusion) | data formatting | bytes 16777216
  256.6 0.9 copy-done.2
  257.5 2.7 scatter_custom_fusion.2
  260.1 6.1 %all-to-all-start.8 = ((f32[64,16,128]{2,1,0:T(8,128)}), f32[64,16,128]{2,1,0:T(8,128)S(1)}, u32[]{:S(2)}, u32[]{:S(2)}) async-start(f32[64,16,128]{2,1,0:T(8,128)} %bitcast.28), calls=%async_computation.10 | async-start | bytes 1048576 | tf_op jit(solution)/shard_map/all_to_all | solution.py:23
  266.3 2.5 scatter_custom_fusion
  268.8 14.3 %all-to-all-done.8 = f32[64,16,128]{2,1,0:T(8,128)S(1)} async-done(((f32[64,16,128]{2,1,0:T(8,128)}), f32[64,16,128]{2,1,0:T(8,128)S(1)}, u32[]{:S(2)}, u32[]{:S(2)}) %all-to-all-start.8) | async-done | bytes 524320 | tf_op jit(solution)/shard_map/all_to_all | solution.py:23
  283.1 6.6 %all-to-all-start.7 = ((f32[64,16,128]{2,1,0:T(8,128)}), f32[64,16,128]{2,1,0:T(8,128)S(1)}, u32[]{:S(2)}, u32[]{:S(2)}) async-start(f32[64,16,128]{2,1,0:T(8,128)} %bitcast.23), calls=%async_computation.9 | async-start | bytes 1048576 | tf_op jit(solution)/shard_map/all_to_all | solution.py:23
  289.6 2.7 scatter_custom_fusion.4
  292.4 14.1 %all-to-all-done.7 = f32[64,16,128]{2,1,0:T(8,128)S(1)} async-done(((f32[64,16,128]{2,1,0:T(8,128)}), f32[64,16,128]{2,1,0:T(8,128)S(1)}, u32[]{:S(2)}, u32[]{:S(2)}) %all-to-all-start.7) | async-done | bytes 524320 | tf_op jit(solution)/shard_map/all_to_all | solution.py:23
  306.5 6.8 %all-to-all-start.9 = ((f32[64,16,128]{2,1,0:T(8,128)}), f32[64,16,128]{2,1,0:T(8,128)S(1)}, u32[]{:S(2)}, u32[]{:S(2)}) async-start(f32[64,16,128]{2,1,0:T(8,128)} %bitcast.33), calls=%async_computation.11 | async-start | bytes 1048576 | tf_op jit(solution)/shard_map/all_to_all | solution.py:23
  313.2 0.5 broadcast.243
  313.8 0.7 reduce.15
  314.5 0.1 reshape.267
  314.6 0.7 reduce.16
  315.4 0.7 reduce.17
  316.1 0.1 reshape.273
  316.3 6.8 %scatter_custom_fusion.1 = f32[3072,128]{1,0:T(8,128)S(1)} fusion(s32[1024]{0:T(1024)S(1)} %bitcast.97, f32[1024,128]{1,0:T(8,128)} %bitcast.82, f32[]{:T(128)} %constant.79.clone.1), kind=kCustom, calls=%fused_computation.22 | custom fusion | flops 131072 | bytes 1573376 | tf_op jit(solution)/shard_map/scatter-add | solution.py:82
  323.1 6.6 %scatter_fusion = f32[3072,128]{1,0:T(8,128)S(1)} fusion(f32[3072,128]{1,0:T(8,128)S(1)} %scatter_custom_fusion.1, s32[1024]{0:T(1024)S(1)} %bitcast.96, f32[1024,128]{1,0:T(8,128)S(1)} %bitcast.77), kind=kCustom, calls=%fused_computation.9 | custom fusion | flops 131072 | bytes 1576960 | tf_op jit(solution)/shard_map/scatter-add | solution.py:82
  329.7 1.7 all-to-all-done.9
  331.4 6.6 %scatter_fusion.1 = f32[3072,128]{1,0:T(8,128)S(1)} fusion(f32[3072,128]{1,0:T(8,128)S(1)} %scatter_fusion, s32[1024]{0:T(1024)S(1)} %bitcast.95, f32[1024,128]{1,0:T(8,128)S(1)} %bitcast.78), kind=kCustom, calls=%fused_computation.11 | custom fusion | flops 131072 | bytes 1576960 | tf_op jit(solution)/shard_map/scatter-add | solution.py:82
  338.1 38.5 %reduce-scatter.8.cloned.1.call-done = f32[8,512]{1,0:T(8,128)} async-done(((f32[512,512]{1,0:T(8,128)}), f32[8,512]{1,0:T(8,128)}) %reduce-scatter.8.cloned.1.call-update) | async-done | bytes 16400 | tf_op jit(solution)/shard_map/reduce_scatter | solution.py:91
  376.5 155.4 %reduce-scatter.10.cloned.1.call-done = f32[64,512]{1,0:T(8,128)} async-done(((f32[4096,512]{1,0:T(8,128)}), f32[64,512]{1,0:T(8,128)}) %reduce-scatter.10.cloned.1.call-update) | async-done | bytes 131088
  (61 shorter events, 0.9 us)
Async XLA Ops:
  7.2 56.3 %copy-start = (bf16[3,1024,128]{2,1,0:T(8,128)(2,1)S(1)}, bf16[3,1024,128]{2,1,0:T(8,128)(2,1)}, u32[]{:S(2)}) copy-start(bf16[3,1024,128]{2,1,0:T(8,128)(2,1)} %param.13) | copy-start | bytes 2359300
  7.2 60.5 %all-gather.3.cloned.1.call-start = ((), (), s32[]{:S(2)}) async-start(), calls=%async_computation.13 | async-start | bytes 5242880 | tf_op jit(solution)/shard_map/all_gather | solution.py:32
  7.9 137.6 %all-gather.5.cloned.1.call-start = ((), (), s32[]{:S(2)}) async-start(), calls=%async_computation.14 | async-start | bytes 4259840 | tf_op jit(solution)/shard_map/all_gather | solution.py:35
  22.2 21.2 %all-to-all-start.5 = ((s32[64,1,16]{2,1,0:T(1,128)}), s32[64,1,16]{2,1,0:T(1,128)S(1)}, u32[]{:S(2)}, u32[]{:S(2)}) async-start(s32[64,1,16]{2,1,0:T(1,128)} %bitcast.15), calls=%async_computation.6 | async-start | bytes 65536 | tf_op jit(solution)/shard_map/all_to_all | solution.py:15
  43.4 13.8 %all-to-all-start.3 = ((s32[64,1,16]{2,1,0:T(1,128)}), s32[64,1,16]{2,1,0:T(1,128)S(1)}, u32[]{:S(2)}, u32[]{:S(2)}) async-start(s32[64,1,16]{2,1,0:T(1,128)} %bitcast.10), calls=%async_computation.4 | async-start | bytes 65536 | tf_op jit(solution)/shard_map/all_to_all | solution.py:15
  58.8 92.6 %all-to-all-start = ((bf16[64,8,512]{2,1,0:T(8,128)(2,1)}), bf16[64,8,512]{2,1,0:T(8,128)(2,1)S(1)}, u32[]{:S(2)}, u32[]{:S(2)}) async-start(bf16[64,8,512]{2,1,0:T(8,128)(2,1)} %stack.2), calls=%async_computation | async-start | bytes 1048576 | tf_op jit(solution)/shard_map/all_to_all | solution.py:41
  151.3 15.7 %copy-start.5 = (f32[512,512]{1,0:T(8,128)}, f32[512,512]{1,0:T(8,128)S(1)}, u32[]{:S(2)}) copy-start(f32[512,512]{1,0:T(8,128)S(1)} %fusion.30) | copy-start | bytes 3145732
  151.3 15.6 %all-to-all-start.1 = ((s32[64,1,16]{2,1,0:T(1,128)}), s32[64,1,16]{2,1,0:T(1,128)S(1)}, u32[]{:S(2)}, u32[]{:S(2)}) async-start(s32[64,1,16]{2,1,0:T(1,128)} %bitcast.4), calls=%async_computation.2 | async-start | bytes 65536 | tf_op jit(solution)/shard_map/all_to_all | solution.py:15
  157.7 62.9 %reduce-scatter.6.cloned.1.call-start = ((), (), s32[]{:S(2)}) async-start(), calls=%async_computation.15 | async-start | bytes 1310720 | tf_op jit(solution)/shard_map/reduce_scatter | solution.py:46
  167.0 16.5 %all-to-all-start.6 = ((bf16[64,16,128]{2,1,0:T(8,128)(2,1)}), bf16[64,16,128]{2,1,0:T(8,128)(2,1)S(1)}, u32[]{:S(2)}, u32[]{:S(2)}) async-start(bf16[64,16,128]{2,1,0:T(8,128)(2,1)} %broadcast_select_fusion), calls=%async_computation.7 | async-start | bytes 524288 | tf_op jit(solution)/shard_map/all_to_all | solution.py:19
  174.9 45.7 %copy-start.4 = (bf16[512,128]{1,0:T(8,128)(2,1)S(1)}, bf16[512,128]{1,0:T(8,128)(2,1)}, u32[]{:S(2)}) copy-start(bf16[512,128]{1,0:T(8,128)(2,1)} %param.15) | copy-start | bytes 393220
  183.5 17.9 %all-to-all-start.4 = ((bf16[64,16,128]{2,1,0:T(8,128)(2,1)}), bf16[64,16,128]{2,1,0:T(8,128)(2,1)S(1)}, u32[]{:S(2)}, u32[]{:S(2)}) async-start(bf16[64,16,128]{2,1,0:T(8,128)(2,1)} %broadcast_select_fusion.1), calls=%async_computation.5 | async-start | bytes 524288 | tf_op jit(solution)/shard_map/all_to_all | solution.py:19
  201.4 17.9 %all-to-all-start.2 = ((bf16[64,16,128]{2,1,0:T(8,128)(2,1)}), bf16[64,16,128]{2,1,0:T(8,128)(2,1)S(1)}, u32[]{:S(2)}, u32[]{:S(2)}) async-start(bf16[64,16,128]{2,1,0:T(8,128)(2,1)} %broadcast_select_fusion.2), calls=%async_computation.3 | async-start | bytes 524288 | tf_op jit(solution)/shard_map/all_to_all | solution.py:19
  207.4 169.2 %reduce-scatter.8.cloned.1.call-start = ((), (), s32[]{:S(2)}) async-start(), calls=%async_computation.16 | async-start | bytes 1064960 | tf_op jit(solution)/shard_map/reduce_scatter | solution.py:91
  221.9 17.3 %copy-start.6 = (f32[512,512]{1,0:T(8,128)S(1)}, f32[512,512]{1,0:T(8,128)}, u32[]{:S(2)}) copy-start(f32[512,512]{1,0:T(8,128)} %copy-done.5) | copy-start | bytes 3145732
  239.2 292.8 %reduce-scatter.10.cloned.1.call-start = ((), (), s32[]{:S(2)}) async-start(), calls=%async_computation.17 | async-start | bytes 8519680
  256.5 1.0 copy-start.2
  260.1 22.9 %all-to-all-start.8 = ((f32[64,16,128]{2,1,0:T(8,128)}), f32[64,16,128]{2,1,0:T(8,128)S(1)}, u32[]{:S(2)}, u32[]{:S(2)}) async-start(f32[64,16,128]{2,1,0:T(8,128)} %bitcast.28), calls=%async_computation.10 | async-start | bytes 1048576 | tf_op jit(solution)/shard_map/all_to_all | solution.py:23
  283.1 23.4 %all-to-all-start.7 = ((f32[64,16,128]{2,1,0:T(8,128)}), f32[64,16,128]{2,1,0:T(8,128)S(1)}, u32[]{:S(2)}, u32[]{:S(2)}) async-start(f32[64,16,128]{2,1,0:T(8,128)} %bitcast.23), calls=%async_computation.9 | async-start | bytes 1048576 | tf_op jit(solution)/shard_map/all_to_all | solution.py:23
  306.5 9.8 %copy-start.3 = (f32[64,16,128]{2,1,0:T(8,128)}, f32[64,16,128]{2,1,0:T(8,128)S(1)}, u32[]{:S(2)}) copy-start(f32[64,16,128]{2,1,0:T(8,128)S(1)} %all-to-all-done.7) | copy-start | bytes 1572868
  306.5 25.0 %all-to-all-start.9 = ((f32[64,16,128]{2,1,0:T(8,128)}), f32[64,16,128]{2,1,0:T(8,128)S(1)}, u32[]{:S(2)}, u32[]{:S(2)}) async-start(f32[64,16,128]{2,1,0:T(8,128)} %bitcast.33), calls=%async_computation.11 | async-start | bytes 1048576 | tf_op jit(solution)/shard_map/all_to_all | solution.py:23
  338.1 193.9 %copy-start.1 = (f32[3072,128]{1,0:T(8,128)}, f32[3072,128]{1,0:T(8,128)S(1)}, u32[]{:S(2)}) copy-start(f32[3072,128]{1,0:T(8,128)S(1)} %scatter_fusion.1) | copy-start | bytes 4718596
Sparse Core Ops, SparseCore 0:
  9.8 53.0 all-gather.2
  65.6 79.8 all-gather.4
  161.6 24.8 reduce-scatter.5
  239.3 137.2 reduce-scatter.7
  381.2 150.7 reduce-scatter.9
